TPU v7x, 32 devices: a whole 2x2x4 slice. The times are simulated.
32 devices in a mesh: ctx: 16 (over z, y, core), kvh: 2 (over x).
Axes of the slice: x: 2, y: 2, z: 4, core: 2. Of those that a mesh axis runs over, the one named last changes fastest.
Arguments:
- queries: bfloat16 [4096, 2048], P(('ctx', 'kvh')), may hold values from -6 to 6
- keys: bfloat16 [4096, 256], P(('ctx', 'kvh')), may hold values from -8 to 8
- values: bfloat16 [4096, 256], P(('ctx', 'kvh')), may hold values from -6 to 6
- grad_out: bfloat16 [4096, 2048], P(('ctx', 'kvh')), may hold values from -6 to 6
- doc_lengths: int32 [8], replicated, may hold values from 1 to 1024, 4096 in all
Outputs:
- attended: bfloat16 [4096, 2048], P(('ctx', 'kvh'))
- grad_queries: bfloat16 [4096, 2048], P(('ctx', 'kvh'))
- grad_keys: bfloat16 [4096, 256], P(('ctx', 'kvh'))
- grad_values: bfloat16 [4096, 256], P(('ctx', 'kvh'))
Inputs may be any that keep to these rules, and one draw needn't show every extreme that they name: `doc_lengths`: 8 lengths that sum to 4096; the longest is exactly 1024.
All inputs are finite; a program needn't handle non-finite values.
Results may differ from a plain program's by a relative error of at most 0.0076.
Values may be sent and summed in bfloat16 or wider, within the bound.
A program may use at most 64 MiB of HBM per device.

v0:
```python
import math

import jax
import jax.numpy as jnp
from jax import lax
from jax.sharding import PartitionSpec as P

REACH = 4


neg_large = -1e30


def from_behind(shard, axis, by):
    peers = lax.axis_size(axis)
    pairs = [(i, i + by) for i in range(peers) if 0 <= i + by < peers]
    return lax.ppermute(shard, axis, pairs)


def document_first(doc_lengths, positions):
    doc_ends = jnp.cumsum(doc_lengths)
    starts = doc_ends - doc_lengths
    before_row = starts[None, :] <= positions[:, None]
    return jnp.max(jnp.where(before_row, starts[None, :], 0), axis=1)


def on_device(queries, keys, values, grad_out, doc_lengths):
    local_queries, local_keys, local_values, local_grads = (
        lax.all_to_all(queries, "kvh", split_axis=1, concat_axis=0, tiled=True),
        lax.all_to_all(keys, "kvh", split_axis=1, concat_axis=0, tiled=True),
        lax.all_to_all(values, "kvh", split_axis=1, concat_axis=0, tiled=True),
        lax.all_to_all(grad_out, "kvh", split_axis=1, concat_axis=0, tiled=True),
    )
    tok_rows = local_queries.shape[0]
    head_width = local_keys.shape[1]
    groups = local_queries.shape[1] // head_width
    scale_factor = 1.0 / math.sqrt(head_width)
    query_heads = local_queries.reshape(tok_rows, groups, head_width)
    grad_heads = local_grads.reshape(tok_rows, groups, head_width)
    first_row = lax.axis_index("ctx") * tok_rows
    offsets = jnp.arange(tok_rows, dtype=jnp.int32)
    query_pos = first_row + offsets
    doc_first = document_first(doc_lengths, query_pos)
    kv_own = jnp.concatenate([local_keys, local_values], axis=1)
    pieces = [kv_own] + [from_behind(kv_own, "ctx", distance) for distance in range(1, REACH + 1)]
    kv_tiles = jnp.stack(pieces)

    def reaches(distance):
        return doc_first[0] <= first_row - (distance - 1) * tok_rows - 1

    def scores_for(distance):
        kv_tile = lax.dynamic_index_in_dim(kv_tiles, distance, 0, keepdims=False)
        key_pos = first_row - distance * tok_rows + offsets
        scores = (
            jnp.einsum(
                "qhd,kd->hqk",
                query_heads,
                kv_tile[:, :head_width],
                preferred_element_type=jnp.float32,
            )
            * scale_factor
        )
        allowed = (key_pos[None, :] >= doc_first[:, None]) & (
            key_pos[None, :] <= query_pos[:, None]
        )
        return (kv_tile, scores, allowed)

    def gather_max(distance, loop_state):

        def gather_compute(partial_state):
            row_max, row_total = partial_state
            _, scores, allowed = scores_for(distance)
            masked = jnp.where(allowed[None], scores, neg_large)
            new_max = jnp.maximum(row_max, masked.max(axis=2))
            row_total = row_total * jnp.exp(row_max - new_max) + jnp.sum(
                jnp.where(allowed[None], jnp.exp(masked - new_max[:, :, None]), 0.0), axis=2
            )
            return (new_max, row_total)

        return lax.cond(reaches(distance), gather_compute, lambda unchanged: unchanged, loop_state)

    start_state = (
        jnp.full((groups, tok_rows), neg_large, jnp.float32),
        jnp.zeros((groups, tok_rows), jnp.float32),
    )
    row_max, row_total = lax.fori_loop(0, REACH + 1, gather_max, start_state)
    log_total = row_max + jnp.log(row_total)

    def weights_for(scores, allowed):
        weights = jnp.where(allowed[None], jnp.exp(scores - log_total[:, :, None]), 0.0).astype(
            jnp.bfloat16
        )
        return lax.optimization_barrier(weights)

    def add_out(distance, summed):

        def add_compute(partial_state):
            kv_tile, scores, allowed = scores_for(distance)
            weights = weights_for(scores, allowed)
            return partial_state + jnp.einsum(
                "hqk,kd->qhd", weights, kv_tile[:, head_width:], preferred_element_type=jnp.float32
            )

        return lax.cond(reaches(distance), add_compute, lambda unchanged: unchanged, summed)

    out_sum = lax.fori_loop(
        0, REACH + 1, add_out, jnp.zeros((tok_rows, groups, head_width), jnp.float32)
    )
    attended = out_sum.astype(jnp.bfloat16).reshape(tok_rows, groups * head_width)
    kept_out = lax.optimization_barrier(attended)
    delta_rows = jnp.sum(
        grad_heads.astype(jnp.float32)
        * kept_out.reshape(tok_rows, groups, head_width).astype(jnp.float32),
        axis=2,
    ).T

    def backward(distance, loop_state):

        def backward_compute(partial_state):
            grad_query, partials = partial_state
            kv_tile, scores, allowed = scores_for(distance)
            weights = weights_for(scores, allowed)
            grad_probs = jnp.einsum(
                "qhd,kd->hqk",
                grad_heads,
                kv_tile[:, head_width:],
                preferred_element_type=jnp.float32,
            )
            grad_scores = (
                weights.astype(jnp.float32) * (grad_probs - delta_rows[:, :, None]) * scale_factor
            ).astype(jnp.bfloat16)
            grad_query = grad_query + jnp.einsum(
                "hqk,kd->qhd",
                grad_scores,
                kv_tile[:, :head_width],
                preferred_element_type=jnp.float32,
            )
            grad_keys = jnp.einsum(
                "hqk,qhd->kd", grad_scores, query_heads, preferred_element_type=jnp.float32
            )
            grad_values = jnp.einsum(
                "hqk,qhd->kd", weights, grad_heads, preferred_element_type=jnp.float32
            )
            partials = lax.dynamic_update_index_in_dim(
                partials, jnp.concatenate([grad_keys, grad_values], axis=1), distance, 0
            )
            return (grad_query, partials)

        return lax.cond(
            reaches(distance), backward_compute, lambda unchanged: unchanged, loop_state
        )

    start_back = (
        jnp.zeros((tok_rows, groups, head_width), jnp.float32),
        jnp.zeros((REACH + 1, tok_rows, 2 * head_width), jnp.float32),
    )
    grad_query, partials = lax.fori_loop(0, REACH + 1, backward, start_back)
    returned = partials[0]
    for distance in range(1, REACH + 1):
        returned = returned + from_behind(partials[distance], "ctx", -distance)
    grad_key_rows = returned[:, :head_width].astype(jnp.bfloat16)
    grad_value_rows = returned[:, head_width:].astype(jnp.bfloat16)
    grad_query_rows = grad_query.astype(jnp.bfloat16).reshape(tok_rows, groups * head_width)
    return (
        lax.all_to_all(attended, "kvh", split_axis=0, concat_axis=1, tiled=True),
        lax.all_to_all(grad_query_rows, "kvh", split_axis=0, concat_axis=1, tiled=True),
        lax.all_to_all(grad_key_rows, "kvh", split_axis=0, concat_axis=1, tiled=True),
        lax.all_to_all(grad_value_rows, "kvh", split_axis=0, concat_axis=1, tiled=True),
    )


def solution(mesh):
    return jax.shard_map(
        on_device,
        mesh=mesh,
        in_specs=(
            P(("ctx", "kvh"), None),
            P(("ctx", "kvh"), None),
            P(("ctx", "kvh"), None),
            P(("ctx", "kvh"), None),
            P(),
        ),
        out_specs=(
            P(("ctx", "kvh"), None),
            P(("ctx", "kvh"), None),
            P(("ctx", "kvh"), None),
            P(("ctx", "kvh"), None),
        ),
        check_vma=False,
    )
```

profile of v0, /device:TPU:20, one launch (start us, length us, event | category | flops | bytes accessed | tf_op | source)
XLA Modules:
  0.0 137.4 jit_solution(15442579911972420318)
XLA Ops:
  2.1 3.3 %all-to-all-start = ((bf16[128,2,128]{2,0,1:T(8,128)(2,1)}), bf16[128,2,128]{2,0,1:T(8,128)(2,1)S(1)}, u32[]{:S(2)}, u32[]{:S(2)}) async-start(bf16[128,2,128]{2,0,1:T(8,128)(2,1)} %copy_bitcast_fusion.1), calls=%async_computation | async-start | bytes 131072 | tf_op jit(solution)/shard_map/all_to_all | solution.py:30
  5.4 1.5 %copy_bitcast_fusion = bf16[128,2,128]{2,0,1:T(8,128)(2,1)} fusion(bf16[128,256]{1,0:T(8,128)(2,1)} %param.19), kind=kLoop, calls=%fused_computation.65 | loop fusion | bytes 131072 | tf_op jit(solution)/shard_map/all_to_all | solution.py:31
  9.5 3.3 %all-to-all-start.1 = ((bf16[128,2,128]{2,0,1:T(8,128)(2,1)}), bf16[128,2,128]{2,0,1:T(8,128)(2,1)S(1)}, u32[]{:S(2)}, u32[]{:S(2)}) async-start(bf16[128,2,128]{2,0,1:T(8,128)(2,1)} %copy_bitcast_fusion), calls=%async_computation.1 | async-start | bytes 131072 | tf_op jit(solution)/shard_map/all_to_all | solution.py:31
  12.8 2.0 %copy.116 = bf16[128,2048]{0,1:T(8,128)(2,1)} copy(bf16[128,2048]{1,0:T(8,128)(2,1)} %param.17) | data formatting | bytes 1048576 | tf_op args[0]
  14.9 2.1 %all-to-all-done.1 = bf16[128,2,128]{2,0,1:T(8,128)(2,1)S(1)} async-done(((bf16[128,2,128]{2,0,1:T(8,128)(2,1)}), bf16[128,2,128]{2,0,1:T(8,128)(2,1)S(1)}, u32[]{:S(2)}, u32[]{:S(2)}) %all-to-all-start.1) | async-done | bytes 65568 | tf_op jit(solution)/shard_map/all_to_all | solution.py:31
  16.9 3.5 %all-to-all-start.2 = ((bf16[128,2,1024]{0,2,1:T(8,128)(2,1)}), bf16[128,2,1024]{0,2,1:T(8,128)(2,1)S(1)}, u32[]{:S(2)}, u32[]{:S(2)}) async-start(bf16[128,2,1024]{0,2,1:T(8,128)(2,1)} %bitcast.29), calls=%async_computation.2 | async-start | bytes 1048576 | tf_op jit(solution)/shard_map/all_to_all | solution.py:29
  20.5 1.9 %collective-permute-start = (bf16[256,256]{1,0:T(8,128)(2,1)S(1)}, bf16[256,256]{1,0:T(8,128)(2,1)S(1)}, u32[]{:S(2)}, u32[]{:S(2)}) collective-permute-start(bf16[256,256]{1,0:T(8,128)(2,1)S(1)} %pad_maximum_fusion), channel_id=1, source_target_pairs={{0,2},{2,4},{4,6},{6,8},{8,10},{10,12},{12,14},{14,16},{16,18},{18... | collective-permute-start | bytes 393224 | tf_op jit(solution)/shard_map/ppermute | solution.py:17
  23.5 4.6 %collective-permute-start.2 = (bf16[256,256]{1,0:T(8,128)(2,1)S(1)}, bf16[256,256]{1,0:T(8,128)(2,1)S(1)}, u32[]{:S(2)}, u32[]{:S(2)}) collective-permute-start(bf16[256,256]{1,0:T(8,128)(2,1)S(1)} %pad_maximum_fusion), channel_id=1, source_target_pairs={{0,6},{2,8},{4,10},{6,12},{8,14},{10,16},{12,18},{14,20},{16,22},{... | collective-permute-start | bytes 393224 | tf_op jit(solution)/shard_map/ppermute | solution.py:17
  28.1 1.9 %collective-permute-start.1 = (bf16[256,256]{1,0:T(8,128)(2,1)S(1)}, bf16[256,256]{1,0:T(8,128)(2,1)S(1)}, u32[]{:S(2)}, u32[]{:S(2)}) collective-permute-start(bf16[256,256]{1,0:T(8,128)(2,1)S(1)} %pad_maximum_fusion), channel_id=1, source_target_pairs={{0,4},{2,6},{4,8},{6,10},{8,12},{10,14},{12,16},{14,18},{16,20},{1... | collective-permute-start | bytes 393224 | tf_op jit(solution)/shard_map/ppermute | solution.py:17
  30.1 1.9 %collective-permute-start.3 = (bf16[256,256]{1,0:T(8,128)(2,1)S(1)}, bf16[256,256]{1,0:T(8,128)(2,1)S(1)}, u32[]{:S(2)}, u32[]{:S(2)}) collective-permute-start(bf16[256,256]{1,0:T(8,128)(2,1)S(1)} %pad_maximum_fusion), channel_id=1, source_target_pairs={{0,8},{2,10},{4,12},{6,14},{8,16},{10,18},{12,20},{14,22},{16,24},... | collective-permute-start | bytes 393224 | tf_op jit(solution)/shard_map/ppermute | solution.py:17
  32.0 3.0 %collective-permute-done.1 = bf16[256,256]{1,0:T(8,128)(2,1)S(1)} collective-permute-done((bf16[256,256]{1,0:T(8,128)(2,1)S(1)}, bf16[256,256]{1,0:T(8,128)(2,1)S(1)}, u32[]{:S(2)}, u32[]{:S(2)}) %collective-permute-start.1) | collective-permute-done | bytes 131104 | tf_op jit(solution)/shard_map/ppermute | solution.py:17
  35.0 3.5 %all-to-all-start.4 = ((bf16[128,2,1024]{0,2,1:T(8,128)(2,1)}), bf16[128,2,1024]{0,2,1:T(8,128)(2,1)S(1)}, u32[]{:S(2)}, u32[]{:S(2)}) async-start(bf16[128,2,1024]{0,2,1:T(8,128)(2,1)} %bitcast.33), calls=%async_computation.4 | async-start | bytes 1048576 | tf_op jit(solution)/shard_map/all_to_all | solution.py:32
  39.3 11.0 %while.61 = (s32[]{:T(128)}, f32[8,256]{1,0:T(8,128)S(1)}, f32[8,256]{1,0:T(8,128)S(1)}, s32[256]{0:T(256)S(1)}, s32[]{:T(128)}, /*index=5*/bf16[5,256,256]{2,1,...) while((s32[]{:T(128)}, f32[8,256]{1,0:T(8,128)S(1)}, ...), condition=%wide.region_7.8_spmd.clone.clone, body=%wide.region_2.7_spmd.clone.clone.sunk | while | flops 138613248 | bytes 5357937 | solution.py:86
  45.4 1.2 conditional.12
  51.5 10.6 %while.62 = (s32[]{:T(128)}, f32[256,8,128]{0,2,1:T(8,128)S(1)}, s32[256]{0:T(256)S(1)}, s32[]{:T(128)}, bf16[5,256,256]{2,1,0:T(8,128)(2,1)S(1)}, /*index=5*/bf...) while((s32[]{:T(128)}, f32[256,8,128]{0,2,1:T(8,128)S(1)}, ...), condition=%wide.region_11.12_spmd.clone.clone, body=%wide.region_8.11_spmd.clone.clone.sunk | while | flops 270991872 | bytes 5259601 | solution.py:106
  65.2 3.5 %all-to-all-start.3 = ((bf16[2,128,1024]{2,1,0:T(8,128)(2,1)}), bf16[2,128,1024]{2,1,0:T(8,128)(2,1)S(1)}, u32[]{:S(2)}, u32[]{:S(2)}) async-start(bf16[2,128,1024]{2,1,0:T(8,128)(2,1)} %copy.148), calls=%async_computation.3 | async-start | bytes 1048576 | tf_op jit(solution)/shard_map/all_to_all | solution.py:165
  70.0 19.2 %while.63 = (s32[]{:T(128)}, f32[256,8,128]{0,2,1:T(8,128)S(1)}, f32[5,256,256]{1,2,0:T(8,128)}, s32[256]{0:T(256)S(1)}, s32[]{:T(128)}, /*index=5*/bf16[5,256,2...) while((s32[]{:T(128)}, f32[256,8,128]{0,2,1:T(8,128)S(1)}, ...), condition=%wide.region_16.17_spmd.clone.clone, body=%wide.region_13.16_spmd.clone.clone.sunk | while | flops 676332032 | bytes 11887013 | solution.py:157
  71.1 3.3 %conditional.14 = ((f32[256,8,128]{0,2,1:T(8,128)S(1)}, f32[5,256,256]{1,2,0:T(8,128)})) conditional(s32[]{:T(128)} %convert_element_type.85, (f32[256,8,128]{0,2,1:T(8,128)S(1)}, f32[5,256,256]{1,2,0:T(8,128)}) %tuple.199, (s32[]{:T(128)}, bf16[5,256,256]{2,1,0:T(8,128)(2,1)S(1)}, s32[]{:T(128)}, s32[256]{0:T(256)S(1)}, s32[256]{0:T(256)S(1)}, ...), branch_computations={%region_14.14_spmd, %region_15.15_spmd} | conditional | flops 676332032 | bytes 11885666 | solution.py:149
  75.6 3.3 %conditional.14 = ((f32[256,8,128]{0,2,1:T(8,128)S(1)}, f32[5,256,256]{1,2,0:T(8,128)})) conditional(s32[]{:T(128)} %convert_element_type.85, (f32[256,8,128]{0,2,1:T(8,128)S(1)}, f32[5,256,256]{1,2,0:T(8,128)}) %tuple.199, (s32[]{:T(128)}, bf16[5,256,256]{2,1,0:T(8,128)(2,1)S(1)}, s32[]{:T(128)}, s32[256]{0:T(256)S(1)}, s32[256]{0:T(256)S(1)}, ...), branch_computations={%region_14.14_spmd, %region_15.15_spmd} | conditional | flops 676332032 | bytes 11885666 | solution.py:149
  80.1 3.3 %conditional.14 = ((f32[256,8,128]{0,2,1:T(8,128)S(1)}, f32[5,256,256]{1,2,0:T(8,128)})) conditional(s32[]{:T(128)} %convert_element_type.85, (f32[256,8,128]{0,2,1:T(8,128)S(1)}, f32[5,256,256]{1,2,0:T(8,128)}) %tuple.199, (s32[]{:T(128)}, bf16[5,256,256]{2,1,0:T(8,128)(2,1)S(1)}, s32[]{:T(128)}, s32[256]{0:T(256)S(1)}, s32[256]{0:T(256)S(1)}, ...), branch_computations={%region_14.14_spmd, %region_15.15_spmd} | conditional | flops 676332032 | bytes 11885666 | solution.py:149
  84.6 3.3 %conditional.14 = ((f32[256,8,128]{0,2,1:T(8,128)S(1)}, f32[5,256,256]{1,2,0:T(8,128)})) conditional(s32[]{:T(128)} %convert_element_type.85, (f32[256,8,128]{0,2,1:T(8,128)S(1)}, f32[5,256,256]{1,2,0:T(8,128)}) %tuple.199, (s32[]{:T(128)}, bf16[5,256,256]{2,1,0:T(8,128)(2,1)S(1)}, s32[]{:T(128)}, s32[256]{0:T(256)S(1)}, s32[256]{0:T(256)S(1)}, ...), branch_computations={%region_14.14_spmd, %region_15.15_spmd} | conditional | flops 676332032 | bytes 11885666 | solution.py:149
  89.1 2.2 %slice_bitcast_fusion.14 = (f32[256,256]{0,1:T(8,128)}, f32[256,256]{0,1:T(8,128)}, f32[256,256]{0,1:T(8,128)}, f32[256,256]{0,1:T(8,128)}) fusion(f32[5,256,256]{1,2,0:T(8,128)} %get-tuple-element.952), kind=kLoop, calls=%fused_computation.58 | loop fusion | bytes 2097152 | tf_op jit(solution)/shard_map/squeeze | solution.py:160
  91.3 1.9 %collective-permute-start.4 = (f32[256,256]{0,1:T(8,128)}, f32[256,256]{0,1:T(8,128)S(1)}, u32[]{:S(2)}, u32[]{:S(2)}) collective-permute-start(f32[256,256]{0,1:T(8,128)} %get-tuple-element.1267), channel_id=1, source_target_pairs={{2,0},{4,2},{6,4},{8,6},{10,8},{12,10},{14,12},{16,14},{18,16},{20... | collective-permute-start | bytes 786440 | tf_op jit(solution)/shard_map/ppermute | solution.py:17
  93.3 1.9 %collective-permute-start.5 = (f32[256,256]{0,1:T(8,128)}, f32[256,256]{0,1:T(8,128)S(1)}, u32[]{:S(2)}, u32[]{:S(2)}) collective-permute-start(f32[256,256]{0,1:T(8,128)} %get-tuple-element.1268), channel_id=1, source_target_pairs={{4,0},{6,2},{8,4},{10,6},{12,8},{14,10},{16,12},{18,14},{20,16},{2... | collective-permute-start | bytes 786440 | tf_op jit(solution)/shard_map/ppermute | solution.py:17
  95.2 4.0 %collective-permute-start.7 = (f32[256,256]{0,1:T(8,128)}, f32[256,256]{0,1:T(8,128)}, u32[]{:S(2)}, u32[]{:S(2)}) collective-permute-start(f32[256,256]{0,1:T(8,128)} %get-tuple-element.1269), channel_id=1, source_target_pairs={{8,0},{10,2},{12,4},{14,6},{16,8},{18,10},{20,12},{22,14},{24,16},... | collective-permute-start | bytes 786440 | tf_op jit(solution)/shard_map/ppermute | solution.py:17
  99.2 1.9 %collective-permute-start.6 = (f32[256,256]{0,1:T(8,128)}, f32[256,256]{0,1:T(8,128)}, u32[]{:S(2)}, u32[]{:S(2)}) collective-permute-start(f32[256,256]{0,1:T(8,128)} %get-tuple-element.1270), channel_id=1, source_target_pairs={{6,0},{8,2},{10,4},{12,6},{14,8},{16,10},{18,12},{20,14},{22,16},{... | collective-permute-start | bytes 786440 | tf_op jit(solution)/shard_map/ppermute | solution.py:17
  102.4 3.5 %all-to-all-start.5 = ((bf16[2,128,1024]{2,1,0:T(8,128)(2,1)}), bf16[2,128,1024]{2,1,0:T(8,128)(2,1)S(1)}, u32[]{:S(2)}, u32[]{:S(2)}) async-start(bf16[2,128,1024]{2,1,0:T(8,128)(2,1)} %copy.149), calls=%async_computation.5 | async-start | bytes 1048576 | tf_op jit(solution)/shard_map/all_to_all | solution.py:166
  105.9 5.5 %collective-permute-done.5 = f32[256,256]{0,1:T(8,128)S(1)} collective-permute-done((f32[256,256]{0,1:T(8,128)}, f32[256,256]{0,1:T(8,128)S(1)}, u32[]{:S(2)}, u32[]{:S(2)}) %collective-permute-start.5) | collective-permute-done | bytes 262176 | tf_op jit(solution)/shard_map/ppermute | solution.py:17
  111.4 8.4 %collective-permute-done.6 = f32[256,256]{0,1:T(8,128)} collective-permute-done((f32[256,256]{0,1:T(8,128)}, f32[256,256]{0,1:T(8,128)}, u32[]{:S(2)}, u32[]{:S(2)}) %collective-permute-start.6) | collective-permute-done | bytes 262176 | tf_op jit(solution)/shard_map/ppermute | solution.py:17
  121.7 3.3 %all-to-all-start.7 = ((bf16[2,128,128]{2,1,0:T(8,128)(2,1)}), bf16[2,128,128]{2,1,0:T(8,128)(2,1)S(1)}, u32[]{:S(2)}, u32[]{:S(2)}) async-start(bf16[2,128,128]{2,1,0:T(8,128)(2,1)} %bitcast.47), calls=%async_computation.7 | async-start | bytes 131072 | tf_op jit(solution)/shard_map/all_to_all | solution.py:168
  125.8 3.4 %all-to-all-done.7 = bf16[2,128,128]{2,1,0:T(8,128)(2,1)S(1)} async-done(((bf16[2,128,128]{2,1,0:T(8,128)(2,1)}), bf16[2,128,128]{2,1,0:T(8,128)(2,1)S(1)}, u32[]{:S(2)}, u32[]{:S(2)}) %all-to-all-start.7) | async-done | bytes 65568 | tf_op jit(solution)/shard_map/all_to_all | solution.py:168
  129.1 3.3 %all-to-all-start.6 = ((bf16[2,128,128]{2,1,0:T(8,128)(2,1)}), bf16[2,128,128]{2,1,0:T(8,128)(2,1)S(1)}, u32[]{:S(2)}, u32[]{:S(2)}) async-start(bf16[2,128,128]{2,1,0:T(8,128)(2,1)} %bitcast.44), calls=%async_computation.6 | async-start | bytes 131072 | tf_op jit(solution)/shard_map/all_to_all | solution.py:167
  (195 shorter events, 58.3 us)
Async XLA Ops:
  0.6 0.8 copy-start
  1.5 21.0 %copy-start.3 = (bf16[128,2048]{1,0:T(8,128)(2,1)S(1)}, bf16[128,2048]{1,0:T(8,128)(2,1)}, u32[]{:S(2)}) copy-start(bf16[128,2048]{1,0:T(8,128)(2,1)} %param.20) | copy-start | bytes 1572868
  2.1 7.4 %all-to-all-start = ((bf16[128,2,128]{2,0,1:T(8,128)(2,1)}), bf16[128,2,128]{2,0,1:T(8,128)(2,1)S(1)}, u32[]{:S(2)}, u32[]{:S(2)}) async-start(bf16[128,2,128]{2,0,1:T(8,128)(2,1)} %copy_bitcast_fusion.1), calls=%async_computation | async-start | bytes 131072 | tf_op jit(solution)/shard_map/all_to_all | solution.py:30
  9.5 7.4 %all-to-all-start.1 = ((bf16[128,2,128]{2,0,1:T(8,128)(2,1)}), bf16[128,2,128]{2,0,1:T(8,128)(2,1)S(1)}, u32[]{:S(2)}, u32[]{:S(2)}) async-start(bf16[128,2,128]{2,0,1:T(8,128)(2,1)} %copy_bitcast_fusion), calls=%async_computation.1 | async-start | bytes 131072 | tf_op jit(solution)/shard_map/all_to_all | solution.py:31
  16.9 18.1 %all-to-all-start.2 = ((bf16[128,2,1024]{0,2,1:T(8,128)(2,1)}), bf16[128,2,1024]{0,2,1:T(8,128)(2,1)S(1)}, u32[]{:S(2)}, u32[]{:S(2)}) async-start(bf16[128,2,1024]{0,2,1:T(8,128)(2,1)} %bitcast.29), calls=%async_computation.2 | async-start | bytes 1048576 | tf_op jit(solution)/shard_map/all_to_all | solution.py:29
  20.5 11.6 %collective-permute-start = (bf16[256,256]{1,0:T(8,128)(2,1)S(1)}, bf16[256,256]{1,0:T(8,128)(2,1)S(1)}, u32[]{:S(2)}, u32[]{:S(2)}) collective-permute-start(bf16[256,256]{1,0:T(8,128)(2,1)S(1)} %pad_maximum_fusion), channel_id=1, source_target_pairs={{0,2},{2,4},{4,6},{6,8},{8,10},{10,12},{12,14},{14,16},{16,18},{18... | collective-permute-start | bytes 393224 | tf_op jit(solution)/shard_map/ppermute | solution.py:17
  23.5 15.0 %collective-permute-start.2 = (bf16[256,256]{1,0:T(8,128)(2,1)S(1)}, bf16[256,256]{1,0:T(8,128)(2,1)S(1)}, u32[]{:S(2)}, u32[]{:S(2)}) collective-permute-start(bf16[256,256]{1,0:T(8,128)(2,1)S(1)} %pad_maximum_fusion), channel_id=1, source_target_pairs={{0,6},{2,8},{4,10},{6,12},{8,14},{10,16},{12,18},{14,20},{16,22},{... | collective-permute-start | bytes 393224 | tf_op jit(solution)/shard_map/ppermute | solution.py:17
  28.1 6.9 %collective-permute-start.1 = (bf16[256,256]{1,0:T(8,128)(2,1)S(1)}, bf16[256,256]{1,0:T(8,128)(2,1)S(1)}, u32[]{:S(2)}, u32[]{:S(2)}) collective-permute-start(bf16[256,256]{1,0:T(8,128)(2,1)S(1)} %pad_maximum_fusion), channel_id=1, source_target_pairs={{0,4},{2,6},{4,8},{6,10},{8,12},{10,14},{12,16},{14,18},{16,20},{1... | collective-permute-start | bytes 393224 | tf_op jit(solution)/shard_map/ppermute | solution.py:17
  30.1 8.5 %collective-permute-start.3 = (bf16[256,256]{1,0:T(8,128)(2,1)S(1)}, bf16[256,256]{1,0:T(8,128)(2,1)S(1)}, u32[]{:S(2)}, u32[]{:S(2)}) collective-permute-start(bf16[256,256]{1,0:T(8,128)(2,1)S(1)} %pad_maximum_fusion), channel_id=1, source_target_pairs={{0,8},{2,10},{4,12},{6,14},{8,16},{10,18},{12,20},{14,22},{16,24},... | collective-permute-start | bytes 393224 | tf_op jit(solution)/shard_map/ppermute | solution.py:17
  35.0 15.3 %all-to-all-start.4 = ((bf16[128,2,1024]{0,2,1:T(8,128)(2,1)}), bf16[128,2,1024]{0,2,1:T(8,128)(2,1)S(1)}, u32[]{:S(2)}, u32[]{:S(2)}) async-start(bf16[128,2,1024]{0,2,1:T(8,128)(2,1)} %bitcast.33), calls=%async_computation.4 | async-start | bytes 1048576 | tf_op jit(solution)/shard_map/all_to_all | solution.py:32
  50.6 0.8 copy-start.1
  62.6 1.0 copy-start.2
  65.2 37.2 %all-to-all-start.3 = ((bf16[2,128,1024]{2,1,0:T(8,128)(2,1)}), bf16[2,128,1024]{2,1,0:T(8,128)(2,1)S(1)}, u32[]{:S(2)}, u32[]{:S(2)}) async-start(bf16[2,128,1024]{2,1,0:T(8,128)(2,1)} %copy.148), calls=%async_computation.3 | async-start | bytes 1048576 | tf_op jit(solution)/shard_map/all_to_all | solution.py:165
  91.3 14.6 %collective-permute-start.4 = (f32[256,256]{0,1:T(8,128)}, f32[256,256]{0,1:T(8,128)S(1)}, u32[]{:S(2)}, u32[]{:S(2)}) collective-permute-start(f32[256,256]{0,1:T(8,128)} %get-tuple-element.1267), channel_id=1, source_target_pairs={{2,0},{4,2},{6,4},{8,6},{10,8},{12,10},{14,12},{16,14},{18,16},{20... | collective-permute-start | bytes 786440 | tf_op jit(solution)/shard_map/ppermute | solution.py:17
  93.3 18.1 %collective-permute-start.5 = (f32[256,256]{0,1:T(8,128)}, f32[256,256]{0,1:T(8,128)S(1)}, u32[]{:S(2)}, u32[]{:S(2)}) collective-permute-start(f32[256,256]{0,1:T(8,128)} %get-tuple-element.1268), channel_id=1, source_target_pairs={{4,0},{6,2},{8,4},{10,6},{12,8},{14,10},{16,12},{18,14},{20,16},{2... | collective-permute-start | bytes 786440 | tf_op jit(solution)/shard_map/ppermute | solution.py:17
  95.2 16.2 %collective-permute-start.7 = (f32[256,256]{0,1:T(8,128)}, f32[256,256]{0,1:T(8,128)}, u32[]{:S(2)}, u32[]{:S(2)}) collective-permute-start(f32[256,256]{0,1:T(8,128)} %get-tuple-element.1269), channel_id=1, source_target_pairs={{8,0},{10,2},{12,4},{14,6},{16,8},{18,10},{20,12},{22,14},{24,16},... | collective-permute-start | bytes 786440 | tf_op jit(solution)/shard_map/ppermute | solution.py:17
  99.2 20.6 %collective-permute-start.6 = (f32[256,256]{0,1:T(8,128)}, f32[256,256]{0,1:T(8,128)}, u32[]{:S(2)}, u32[]{:S(2)}) collective-permute-start(f32[256,256]{0,1:T(8,128)} %get-tuple-element.1270), channel_id=1, source_target_pairs={{6,0},{8,2},{10,4},{12,6},{14,8},{16,10},{18,12},{20,14},{22,16},{... | collective-permute-start | bytes 786440 | tf_op jit(solution)/shard_map/ppermute | solution.py:17
  102.4 19.3 %all-to-all-start.5 = ((bf16[2,128,1024]{2,1,0:T(8,128)(2,1)}), bf16[2,128,1024]{2,1,0:T(8,128)(2,1)S(1)}, u32[]{:S(2)}, u32[]{:S(2)}) async-start(bf16[2,128,1024]{2,1,0:T(8,128)(2,1)} %copy.149), calls=%async_computation.5 | async-start | bytes 1048576 | tf_op jit(solution)/shard_map/all_to_all | solution.py:166
  121.7 7.4 %all-to-all-start.7 = ((bf16[2,128,128]{2,1,0:T(8,128)(2,1)}), bf16[2,128,128]{2,1,0:T(8,128)(2,1)S(1)}, u32[]{:S(2)}, u32[]{:S(2)}) async-start(bf16[2,128,128]{2,1,0:T(8,128)(2,1)} %bitcast.47), calls=%async_computation.7 | async-start | bytes 131072 | tf_op jit(solution)/shard_map/all_to_all | solution.py:168
  129.1 7.4 %all-to-all-start.6 = ((bf16[2,128,128]{2,1,0:T(8,128)(2,1)}), bf16[2,128,128]{2,1,0:T(8,128)(2,1)S(1)}, u32[]{:S(2)}, u32[]{:S(2)}) async-start(bf16[2,128,128]{2,1,0:T(8,128)(2,1)} %bitcast.44), calls=%async_computation.6 | async-start | bytes 131072 | tf_op jit(solution)/shard_map/all_to_all | solution.py:167
where the time goes:
time: 140 us; the launch traced here: 137 us
  starting transfers between devices  47.3 us (34%)
  local copies, waits for them, and re-layouts  28.9 us (21%)
  waiting for transfers between devices  24.1 us (17%)
  matrix products  15 us (11%)
  loops' own time  11.1 us (8%)
  other arithmetic  9.92 us (7%)
    ppermute x8, starting transfers between devices, from_behind(): return lax.ppermute(shard, axis, pairs)  20.1 us
    ppermute x8, waiting for transfers between devices, from_behind(): return lax.ppermute(shard, axis, pairs)  16.9 us
    unnamed x24, local copies, waits for them, and re-layouts  9.78 us
    slice x15, local copies, waits for them, and re-layouts, reaches(): return doc_first[0] <= first_row - (distance - 1) * tok_rows - 1  7.85 us
    dot_general x12, matrix products, scores_for(): jnp.einsum('qhd,kd->hqk', query_heads, kv_tile[:, :head_width], preferred...  6.67 us
    all_to_all x1, starting transfers between devices, on_device(): lax.all_to_all(grad_out, 'kvh', split_axis=1, concat_axis=0, tiled=True)  3.5 us
    all_to_all x1, starting transfers between devices, on_device(): lax.all_to_all(grad_query_rows, 'kvh', split_axis=0, concat_axis=1, tiled...  3.49 us
    all_to_all x1, starting transfers between devices, on_device(): lax.all_to_all(queries, 'kvh', split_axis=1, concat_axis=0, tiled=True)  3.49 us
  transfers between devices with their start and end apart: 16, of which 7 were waited for; matrix products, arithmetic and copies ran while one was open for 29% of the time, Pallas kernels for 0%

commit v1 on v0

v1 whole, which is shorter than its diff:
```python
import functools
import math

import jax
import jax.numpy as jnp
from jax import lax
from jax.experimental import pallas as pl
from jax.experimental.pallas import tpu as pltpu
from jax.sharding import PartitionSpec as P

REACH = 4
LANES = 256
NEG_LARGE = -1e30
F32 = jnp.float32
BF16 = jnp.bfloat16


def matmul(a, b):
    return lax.dot_general(a, b, (((1,), (0,)), ((), ())), preferred_element_type=F32)


def kernel(
    ranges, groups, head_width, doc_ref, q_hbm, k_hbm, v_hbm, do_hbm,
    att_ref, gq_ref, gk_ref, gv_ref,
    q_ref, do_ref, kv_ref, kvt_ref, bias_ref, s_ref, e_ref, acc_ref, out_ref, in_ref,
    load_sem, kv_send, kv_recv, back_send, back_recv,
):
    tokens = q_ref.shape[0]
    reach = REACH * groups
    slots = reach + 1
    window = slots * tokens
    heads = q_ref.shape[1] // head_width // groups
    per_step = LANES // tokens
    steps = heads // per_step
    blocks = ranges * groups
    scale = 1.0 / math.sqrt(head_width)
    scale_2 = scale * math.log2(math.e)
    me = lax.axis_index("ctx") * groups + lax.axis_index("kvh")

    def device(block):
        return (block // groups, block % groups)

    def later(d):
        return pl.when(me + d < blocks)

    def earlier(d):
        return pl.when(me - d >= 0)

    def slot(s):
        return pl.ds(s * tokens, tokens)

    own_loads = []
    for g in range(groups):
        columns = pl.ds(g * head_width, head_width)
        for i, src in enumerate((k_hbm, v_hbm)):
            own_loads.append(
                pltpu.make_async_copy(
                    src.at[:, columns],
                    kv_ref.at[g, slot(reach), pl.ds(i * head_width, head_width)],
                    load_sem.at[2 * g + i],
                )
            )
    big_loads = [
        pltpu.make_async_copy(q_hbm, q_ref, load_sem.at[2 * groups]),
        pltpu.make_async_copy(do_hbm, do_ref, load_sem.at[2 * groups + 1]),
    ]
    for copy in own_loads + big_loads:
        copy.start()

    barrier = pltpu.get_barrier_semaphore()
    for d in range(1, reach + 1):

        @later(d)
        def _():
            pl.semaphore_signal(
                barrier, 1, device_id=device(me + d), device_id_type=pl.DeviceIdType.MESH
            )

        @earlier(d)
        def _():
            pl.semaphore_signal(
                barrier, 1, device_id=device(me - d), device_id_type=pl.DeviceIdType.MESH
            )

    def kv_copy(g, d):
        return pltpu.make_async_remote_copy(
            src_ref=kv_ref.at[g, slot(reach), :],
            dst_ref=kv_ref.at[g, slot(reach - d), :],
            send_sem=kv_send.at[g, d - 1],
            recv_sem=kv_recv.at[g, d - 1],
            device_id=device(me + d),
            device_id_type=pl.DeviceIdType.MESH,
        )

    def back_copy(g, d):
        return pltpu.make_async_remote_copy(
            src_ref=out_ref.at[g, slot(reach - d), :],
            dst_ref=in_ref.at[g, slot(d - 1), :],
            send_sem=back_send.at[g, d - 1],
            recv_sem=back_recv.at[g, d - 1],
            device_id=device(me - d),
            device_id_type=pl.DeviceIdType.MESH,
        )

    pl.semaphore_wait(barrier, jnp.minimum(me, reach) + jnp.minimum(blocks - 1 - me, reach))
    for copy in own_loads:
        copy.wait()
    for g in range(groups):
        for d in range(1, reach + 1):

            @later(d)
            def _():
                kv_copy(g, d).start()

    for d in range(1, reach + 1):

        @pl.when(me - d < 0)
        def _():
            for g in range(groups):
                kv_ref[g, slot(reach - d), :] = jnp.zeros((tokens, 2 * head_width), BF16)

    query_pos = me * tokens + lax.broadcasted_iota(jnp.int32, (8, LANES), 1) % tokens

    def next_doc(i, carry):
        start, first = carry
        first = jnp.where(start <= query_pos, jnp.maximum(first, start), first)
        return start + doc_ref[i], first

    _, doc_first = lax.fori_loop(
        0, doc_ref.shape[0], next_doc, (jnp.int32(0), jnp.zeros((8, LANES), jnp.int32))
    )
    for s in range(slots):
        key_pos = (me - reach + s) * tokens + lax.broadcasted_iota(jnp.int32, (tokens, LANES), 0)
        allowed = (key_pos >= doc_first[0:1]) & (key_pos <= query_pos[0:1])
        bias_ref[slot(s), :] = jnp.where(allowed, 0.0, NEG_LARGE)

    for copy in big_loads:
        copy.wait()

    for g in range(groups):
        for d in range(1, reach + 1):

            @earlier(d)
            def _():
                kv_copy(g, d).wait_recv()

        for s in range(slots):
            kvt_ref[:, slot(s)] = kv_ref[g, slot(s), :].T

        acc_ref[...] = jnp.zeros_like(acc_ref)

        def step(i, carry):
            first_head = g * heads + i * per_step

            def head_columns(j):
                return pl.ds(pl.multiple_of((first_head + j) * head_width, head_width), head_width)

            def stacked(ref):
                return jnp.concatenate([ref[:, head_columns(j)] for j in range(per_step)], axis=0)

            q = stacked(q_ref)
            do = stacked(do_ref)
            q_t = q.T
            do_t = do.T
            top = jnp.full((8, LANES), NEG_LARGE, F32)
            for s in range(slots):
                scores = matmul(kv_ref[g, slot(s), :head_width], q_t) * scale_2 + bias_ref[slot(s), :]
                s_ref[slot(s), :] = scores
                top = jnp.maximum(top, jnp.max(scores.reshape(tokens // 8, 8, LANES), axis=0))
            row_max = jnp.max(top, axis=0, keepdims=True)
            total = jnp.zeros((8, LANES), F32)
            for s in range(slots):
                weights = jnp.exp2(s_ref[slot(s), :] - row_max)
                total = total + jnp.sum(weights.reshape(tokens // 8, 8, LANES), axis=0)
                e_ref[slot(s), :] = weights.astype(BF16)
            inverse = 1.0 / jnp.sum(total, axis=0, keepdims=True)
            out_t = (matmul(kvt_ref[head_width:, :], e_ref[...]) * inverse).astype(BF16)
            delta = jnp.sum(out_t.astype(F32) * do_t.astype(F32), axis=0, keepdims=True)
            out = out_t.T
            scaled_do = (do_t.astype(F32) * inverse).astype(BF16).T
            gq_t = jnp.zeros((head_width, LANES), F32)
            for s in range(slots):
                weights = e_ref[slot(s), :]
                grad_probs = matmul(kv_ref[g, slot(s), head_width:], do_t)
                grad_scores = (weights.astype(F32) * ((grad_probs - delta) * inverse)).astype(BF16)
                gq_t = gq_t + matmul(kvt_ref[:head_width, slot(s)], grad_scores)
                acc_ref[slot(s), :head_width] += matmul(grad_scores, q)
                acc_ref[slot(s), head_width:] += matmul(weights, scaled_do)
            gq = (gq_t * scale).astype(BF16).T
            for j in range(per_step):
                att_ref[:, head_columns(j)] = out[j * tokens:(j + 1) * tokens]
                gq_ref[:, head_columns(j)] = gq[j * tokens:(j + 1) * tokens]
            return carry

        lax.fori_loop(0, steps, step, 0)

        for d in range(1, reach + 1):
            out_ref[g, slot(reach - d), :head_width] = (
                acc_ref[slot(reach - d), :head_width] * scale
            ).astype(BF16)
            out_ref[g, slot(reach - d), head_width:] = acc_ref[slot(reach - d), head_width:].astype(BF16)

            @earlier(d)
            def _():
                back_copy(g, d).start()

        columns = slice(g * head_width, (g + 1) * head_width)
        gk_ref[:, columns] = acc_ref[slot(reach), :head_width] * scale
        gv_ref[:, columns] = acc_ref[slot(reach), head_width:]

    for g in range(groups):
        columns = slice(g * head_width, (g + 1) * head_width)
        for d in range(1, reach + 1):

            @later(d)
            def _():
                back_copy(g, d).wait_recv()
                part = in_ref[g, slot(d - 1), :].astype(F32)
                gk_ref[:, columns] += part[:, :head_width]
                gv_ref[:, columns] += part[:, head_width:]

    for g in range(groups):
        for d in range(1, reach + 1):

            @later(d)
            def _():
                kv_copy(g, d).wait_send()

            @earlier(d)
            def _():
                back_copy(g, d).wait_send()


def on_device(ranges, groups, queries, keys, values, grad_out, doc_lengths):
    tokens = queries.shape[0]
    head_width = keys.shape[1] // groups
    reach = REACH * groups
    window = (reach + 1) * tokens
    anywhere = pl.BlockSpec(memory_space=pl.ANY)
    vmem = pl.BlockSpec(memory_space=pltpu.VMEM)
    dma = pltpu.SemaphoreType.DMA
    attended, grad_queries, grad_keys, grad_values = pl.pallas_call(
        functools.partial(kernel, ranges, groups, head_width),
        out_shape=(
            jax.ShapeDtypeStruct(queries.shape, BF16),
            jax.ShapeDtypeStruct(queries.shape, BF16),
            jax.ShapeDtypeStruct(keys.shape, F32),
            jax.ShapeDtypeStruct(keys.shape, F32),
        ),
        in_specs=[pl.BlockSpec(memory_space=pltpu.SMEM)] + [anywhere] * 4,
        out_specs=[vmem] * 4,
        scratch_shapes=[
            pltpu.VMEM(queries.shape, BF16),
            pltpu.VMEM(queries.shape, BF16),
            pltpu.VMEM((groups, window, 2 * head_width), BF16),
            pltpu.VMEM((2 * head_width, window), BF16),
            pltpu.VMEM((window, LANES), F32),
            pltpu.VMEM((window, LANES), F32),
            pltpu.VMEM((window, LANES), BF16),
            pltpu.VMEM((window, 2 * head_width), F32),
            pltpu.VMEM((groups, window, 2 * head_width), BF16),
            pltpu.VMEM((groups, reach * tokens, 2 * head_width), BF16),
            dma((2 * groups + 2,)),
            dma((groups, reach)),
            dma((groups, reach)),
            dma((groups, reach)),
            dma((groups, reach)),
        ],
        compiler_params=pltpu.CompilerParams(collective_id=0, has_side_effects=True),
    )(doc_lengths, queries, keys, values, grad_out)
    return attended, grad_queries, grad_keys.astype(BF16), grad_values.astype(BF16)


def solution(mesh):
    rows = P(("ctx", "kvh"), None)
    return jax.shard_map(
        functools.partial(on_device, mesh.shape["ctx"], mesh.shape["kvh"]),
        mesh=mesh,
        in_specs=(rows, rows, rows, rows, P()),
        out_specs=(rows, rows, rows, rows),
        check_vma=False,
    )
```

time: 140 us -> 52.1 us (0.37)
  the two profiles are of different devices: /device:TPU:20 before, /device:TPU:16 now
where the time goes in v1:
time: 52.1 us; the launch traced here: 51.9 us
  Pallas kernels  46.3 us (89%)
  local copies, waits for them, and re-layouts  2.74 us (5%)
  other arithmetic  2.21 us (4%)
  between operations  0.65 us (1%)
    pallas_call x1, Pallas kernels, on_device(): pl.pallas_call(functools.partial(kernel, ranges, groups, head_width), out...  46.3 us
    unnamed x6, local copies, waits for them, and re-layouts  2.74 us
    convert_element_type x1, other arithmetic, on_device(): grad_keys.astype(BF16)  1.58 us

profile of v1, /device:TPU:16, one launch (start us, length us, event | category | flops | bytes accessed | tf_op | source)
XLA Modules:
  0.0 51.9 jit_solution(7285639493800827863)
XLA Ops:
  0.6 46.3 %shard_map.84 = (bf16[128,2048]{1,0:T(8,128)(2,1)}, bf16[128,2048]{1,0:T(8,128)(2,1)}, f32[128,256]{1,0:T(8,128)}, f32[128,256]{1,0:T(8,128)}) custom-call(s32[8]{0:T(128)} %doc_ref.1, bf16[128,2048]{1,0:T(8,128)(2,1)} %q_hbm.1, bf16[128,256]{1,0:T(8,128)(2,1)} %k_hbm.1, bf16[128,256]{1,0:T(8,128)(2,1)} %v_hbm.1, bf16[128,2048]{1,0:T(8,128)(2,1)} %do_hbm.1), custom_call_target="tpu_custom_call" | custom-call | tf_op jit(solution)/shard_map/pallas_call | solution.py:242
  46.9 0.0 copy-start.1
  46.9 1.6 %convert_element_type.6 = bf16[128,256]{1,0:T(8,128)(2,1)} convert(f32[128,256]{1,0:T(8,128)} %get-tuple-element.10) | non-fusion elementwise | flops 32768 | bytes 196608 | tf_op jit(solution)/shard_map/convert_element_type | solution.py:271
  48.5 0.0 copy-done.1
  48.5 0.6 %convert_element_type.7 = bf16[128,256]{1,0:T(8,128)(2,1)} convert(f32[128,256]{1,0:T(8,128)S(1)} %copy-done.1) | non-fusion elementwise | flops 32768 | bytes 196608 | tf_op jit(solution)/shard_map/convert_element_type | solution.py:271
  49.2 0.0 copy-start
  49.2 1.9 %copy.11 = bf16[128,2048]{1,0:T(8,128)(2,1)} copy(bf16[128,2048]{1,0:T(8,128)(2,1)} %get-tuple-element.16) | data formatting | bytes 1048576
  51.1 0.0 copy-done
  51.1 0.8 %copy.12 = bf16[128,2048]{1,0:T(8,128)(2,1)} copy(bf16[128,2048]{1,0:T(8,128)(2,1)S(1)} %copy-done) | data formatting | bytes 1048576
Async XLA Ops:
  46.9 1.6 %copy-start.1 = (f32[128,256]{1,0:T(8,128)S(1)}, f32[128,256]{1,0:T(8,128)}, u32[]{:S(2)}) copy-start(f32[128,256]{1,0:T(8,128)} %get-tuple-element.11) | copy-start | bytes 393220
  49.2 1.9 %copy-start = (bf16[128,2048]{1,0:T(8,128)(2,1)S(1)}, bf16[128,2048]{1,0:T(8,128)(2,1)}, u32[]{:S(2)}) copy-start(bf16[128,2048]{1,0:T(8,128)(2,1)} %get-tuple-element.17) | copy-start | bytes 1572868

commit v2 on v1

v2 whole, which is shorter than its diff:
```python
import functools
import math

import jax
import jax.numpy as jnp
from jax import lax
from jax.experimental import pallas as pl
from jax.experimental.pallas import tpu as pltpu
from jax.sharding import PartitionSpec as P

REACH = 4
LANES = 256
SPAN = 3
NEG_LARGE = -1e30
F32 = jnp.float32
BF16 = jnp.bfloat16
MESH = pl.DeviceIdType.MESH


def matmul(a, b):
    return lax.dot_general(a, b, (((1,), (0,)), ((), ())), preferred_element_type=F32)


def kernel(
    ranges, groups, head_width, doc_ref, q_hbm, k_hbm, v_hbm, do_hbm,
    att_ref, gq_ref, gk_out, gv_out,
    q_ref, do_ref, kv_ref, kvt_ref, bias_ref, s_ref, e_ref, acc_ref, out_ref, in_ref, pair_ref, prior_ref, gk_ref, gv_ref,
    load_sem, kv_send, kv_recv, pass_send, back_send, back_recv, pair_recv,
):
    tokens = q_ref.shape[0]
    reach = REACH * groups
    slots = reach + 1
    window = slots * tokens
    heads = q_ref.shape[1] // head_width // groups
    per_step = LANES // tokens
    spans = [
        pl.ds(a * tokens, min(SPAN, slots - a) * tokens) for a in range(0, slots, SPAN)
    ]
    steps = heads // per_step
    blocks = ranges * groups
    scale = 1.0 / math.sqrt(head_width)
    scale_2 = scale * math.log2(math.e)
    me = lax.axis_index("ctx") * groups + lax.axis_index("kvh")

    place = me % reach
    band = me - place
    core = (place // groups) % 2
    chip = place - core * groups
    toward_partner = groups * (1 - 2 * core)

    def device(block):
        return (block // groups, block % groups)

    def both(*conditions):
        held = conditions[0]
        for condition in conditions[1:]:
            held = jnp.logical_and(held, condition)
        return held

    def core_of(at):
        return (at // groups) % 2

    def chip_of(at):
        return at - core_of(at) * groups

    def shared(source, at):
        first = chip_of(at)
        return both(
            chip_of(source) != first,
            jnp.logical_or(source < first, source > first + groups),
        )

    def reached(d):
        target = (place + d) % reach
        relayed = both(core_of(target) != core, shared(place, target))
        own = place + d < reach
        exists = jnp.logical_or(own, band > 0)
        return target, own, both(exists, jnp.logical_not(relayed))

    def source_of(d):
        source = (place - d + reach) % reach
        exists = me - d >= 0
        pair = both(exists, shared(source, place))
        same = core_of(source) == core
        return source, exists, both(pair, same), both(pair, jnp.logical_not(same))

    def slot(s):
        return pl.ds(s * tokens, tokens)

    own_loads = []
    for g in range(groups):
        columns = pl.ds(g * head_width, head_width)
        for i, src in enumerate((k_hbm, v_hbm)):
            own_loads.append(
                pltpu.make_async_copy(
                    src.at[:, columns],
                    kv_ref.at[g, slot(reach), pl.ds(i * head_width, head_width)],
                    load_sem.at[2 * g + i],
                )
            )
    big_loads = [
        pltpu.make_async_copy(q_hbm, q_ref, load_sem.at[2 * groups]),
        pltpu.make_async_copy(do_hbm, do_ref, load_sem.at[2 * groups + 1]),
    ]
    for copy in own_loads + big_loads:
        copy.start()

    barrier = pltpu.get_barrier_semaphore()
    for d in range(1, reach):
        pl.semaphore_signal(
            barrier, 1, device_id=device(band + (place + d) % reach), device_id_type=MESH
        )
    has_next = me + reach < blocks
    has_prior = band > 0

    @pl.when(has_next)
    def _():
        pl.semaphore_signal(barrier, 1, device_id=device(me + reach), device_id_type=MESH)

    @pl.when(has_prior)
    def _():
        pl.semaphore_signal(barrier, 1, device_id=device(me - reach), device_id_type=MESH)

    def send(src, dst, send_sem, recv_sem, block):
        return pltpu.make_async_remote_copy(
            src_ref=src, dst_ref=dst, send_sem=send_sem, recv_sem=recv_sem,
            device_id=device(block), device_id_type=MESH,
        )

    def kv_copy(g, d, source_slot, block):
        return send(
            kv_ref.at[g, slot(source_slot), :], kv_ref.at[g, slot(reach - d), :],
            kv_send.at[g, d - 1], kv_recv.at[g, d - 1], block,
        )

    def kv_pass(g, d):
        other = d + toward_partner
        return send(
            kv_ref.at[g, slot(reach - d), :],
            kv_ref.at[g, pl.ds(pl.multiple_of((reach - other) * tokens, tokens), tokens), :],
            pass_send.at[g, d - 1], kv_recv.at[g, other - 1], me + toward_partner,
        )

    def back_pair(g, d):
        other = d + toward_partner
        return send(
            out_ref.at[g, slot(reach - d), :],
            pair_ref.at[g, pl.ds(pl.multiple_of((other - 1) * tokens, tokens), tokens), :],
            back_send.at[g, d - 1], pair_recv.at[g, other - 1], me + toward_partner,
        )

    def back_copy(g, d):
        block = me - reach if d == reach else band + (place - d + reach) % reach
        return send(
            out_ref.at[g, slot(reach - d), :], in_ref.at[g, slot(d - 1), :],
            back_send.at[g, d - 1], back_recv.at[g, d - 1], block,
        )

    pl.semaphore_wait(
        barrier, reach - 1 + jnp.where(has_next, 1, 0) + jnp.where(has_prior, 1, 0)
    )
    for copy in own_loads:
        copy.wait()
    for g in range(groups):

        @pl.when(has_next)
        def _():
            kv_copy(g, reach, reach, me + reach).start()

        for d in range(1, reach):
            target, own, straight = reached(d)

            @pl.when(both(own, straight))
            def _():
                kv_copy(g, d, reach, band + target).start()

    def forward_prior(g):
        @pl.when(has_prior)
        def _():
            kv_copy(g, reach, reach, me).wait_recv()

        for d in range(1, reach):
            target, own, straight = reached(d)

            @pl.when(both(jnp.logical_not(own), straight))
            def _():
                kv_copy(g, d, 0, band + target).start()

    def relay(g):
        for d in range(1, reach):
            _, _, relays, _ = source_of(d)

            @pl.when(relays)
            def _():
                kv_copy(g, d, reach, me).wait_recv()
                kv_pass(g, d).start()

    def receive(g):
        for d in range(1, reach):
            _, exists, relays, _ = source_of(d)

            @pl.when(both(exists, jnp.logical_not(relays)))
            def _():
                kv_copy(g, d, reach, me).wait_recv()

    def add_rows(target_ref, g, s, part_ref, rows):
        target_ref[g, slot(s), :] = (
            target_ref[g, slot(s), :].astype(F32) + part_ref[g, rows, :].astype(F32)
        ).astype(BF16)

    def send_partials(g):
        for d in range(1, reach):
            _, exists, relays, relayed = source_of(d)

            @pl.when(relayed)
            def _():
                back_pair(g, d).start()

            @pl.when(both(exists, jnp.logical_not(relays), jnp.logical_not(relayed)))
            def _():
                back_copy(g, d).start()

    def send_pair_sums(g):
        for d in range(1, reach):
            _, _, relays, _ = source_of(d)

            @pl.when(relays)
            def _():
                send(
                    out_ref.at[g, slot(reach - d), :], pair_ref.at[g, slot(d - 1), :],
                    back_send.at[g, d - 1], pair_recv.at[g, d - 1], me + toward_partner,
                ).wait_recv()
                add_rows(out_ref, g, reach - d, pair_ref, slot(d - 1))
                back_copy(g, d).start()

    def send_band_sums(g):
        for d in range(1, reach):
            _, own, straight = reached(d)

            @pl.when(both(jnp.logical_not(own), straight))
            def _():
                back_copy(g, d).wait_recv()
                part = in_ref[g, slot(d - 1), :].astype(F32)
                prior_ref[g] += part

        @pl.when(has_prior)
        def _():
            out_ref[g, slot(0), :] = prior_ref[g].astype(BF16)
            back_copy(g, reach).start()

    def collect(g):
        columns = slice(g * head_width, (g + 1) * head_width)

        def add(d):
            back_copy(g, d).wait_recv()
            part = in_ref[g, slot(d - 1), :].astype(F32)
            gk_ref[:, columns] += part[:, :head_width]
            gv_ref[:, columns] += part[:, head_width:]

        for d in range(1, reach):
            _, own, straight = reached(d)

            @pl.when(both(own, straight))
            def _():
                add(d)

        @pl.when(has_next)
        def _():
            add(reach)

    for d in range(1, reach + 1):

        @pl.when(me - d < 0)
        def _():
            for g in range(groups):
                kv_ref[g, slot(reach - d), :] = jnp.zeros((tokens, 2 * head_width), BF16)

    query_pos = me * tokens + lax.broadcasted_iota(jnp.int32, (8, LANES), 1) % tokens

    def next_doc(i, carry):
        start, first = carry
        first = jnp.where(start <= query_pos, jnp.maximum(first, start), first)
        return start + doc_ref[i], first

    _, doc_first = lax.fori_loop(
        0, doc_ref.shape[0], next_doc, (jnp.int32(0), jnp.zeros((8, LANES), jnp.int32))
    )
    for s in range(slots):
        key_pos = (me - reach + s) * tokens + lax.broadcasted_iota(jnp.int32, (tokens, LANES), 0)
        allowed = (key_pos >= doc_first[0:1]) & (key_pos <= query_pos[0:1])
        bias_ref[slot(s), :] = jnp.where(allowed, 0.0, NEG_LARGE)

    for copy in big_loads:
        copy.wait()

    forward_prior(0)
    relay(0)
    if groups > 1:
        forward_prior(1)

    for g in range(groups):
        receive(g)

        for s in range(slots):
            kvt_ref[:, slot(s)] = kv_ref[g, slot(s), :].T

        acc_ref[...] = jnp.zeros_like(acc_ref)

        def step(i, carry):
            first_head = g * heads + i * per_step

            def head_columns(j):
                return pl.ds(pl.multiple_of((first_head + j) * head_width, head_width), head_width)

            def stacked(ref):
                return jnp.concatenate([ref[:, head_columns(j)] for j in range(per_step)], axis=0)

            q = stacked(q_ref)
            do = stacked(do_ref)
            q_t = q.T
            do_t = do.T
            top = jnp.full((8, LANES), NEG_LARGE, F32)
            for rows in spans:
                scores = matmul(kv_ref[g, rows, :head_width], q_t) * scale_2 + bias_ref[rows, :]
                s_ref[rows, :] = scores
                top = jnp.maximum(top, jnp.max(scores.reshape(-1, 8, LANES), axis=0))
            row_max = jnp.max(top, axis=0, keepdims=True)
            total = jnp.zeros((8, LANES), F32)
            for rows in spans:
                weights = jnp.exp2(s_ref[rows, :] - row_max)
                total = total + jnp.sum(weights.reshape(-1, 8, LANES), axis=0)
                e_ref[rows, :] = weights.astype(BF16)
            inverse = 1.0 / jnp.sum(total, axis=0, keepdims=True)
            out_t = (matmul(kvt_ref[head_width:, :], e_ref[...]) * inverse).astype(BF16)
            delta = jnp.sum(out_t.astype(F32) * do_t.astype(F32), axis=0, keepdims=True)
            out = out_t.T
            scaled_do = (do_t.astype(F32) * inverse).astype(BF16).T
            gq_t = jnp.zeros((head_width, LANES), F32)
            for rows in spans:
                weights = e_ref[rows, :]
                grad_probs = matmul(kv_ref[g, rows, head_width:], do_t)
                grad_scores = (weights.astype(F32) * ((grad_probs - delta) * inverse)).astype(BF16)
                gq_t = gq_t + matmul(kvt_ref[:head_width, rows], grad_scores)
                acc_ref[rows, :head_width] += matmul(grad_scores, q)
                acc_ref[rows, head_width:] += matmul(weights, scaled_do)
            gq = (gq_t * scale).astype(BF16).T
            for j in range(per_step):
                att_ref[:, head_columns(j)] = out[j * tokens:(j + 1) * tokens]
                gq_ref[:, head_columns(j)] = gq[j * tokens:(j + 1) * tokens]
            return carry

        lax.fori_loop(0, steps - 1, step, 0)
        if g + 1 < groups:
            relay(g + 1)
        if g + 2 < groups:
            forward_prior(g + 2)
        if g > 0:
            send_pair_sums(g - 1)
        lax.fori_loop(steps - 1, steps, step, 0)
        if g > 0:
            send_band_sums(g - 1)

        for d in range(1, reach):
            out_ref[g, slot(reach - d), :head_width] = (
                acc_ref[slot(reach - d), :head_width] * scale
            ).astype(BF16)
            out_ref[g, slot(reach - d), head_width:] = acc_ref[slot(reach - d), head_width:].astype(BF16)
        send_partials(g)
        prior_ref[g, :, :head_width] = acc_ref[slot(0), :head_width] * scale
        prior_ref[g, :, head_width:] = acc_ref[slot(0), head_width:]
        columns = slice(g * head_width, (g + 1) * head_width)
        gk_ref[:, columns] = acc_ref[slot(reach), :head_width] * scale
        gv_ref[:, columns] = acc_ref[slot(reach), head_width:]

    send_pair_sums(groups - 1)
    send_band_sums(groups - 1)
    for g in range(groups):
        collect(g)
    gk_out[...] = gk_ref[...].astype(BF16)
    gv_out[...] = gv_ref[...].astype(BF16)

    for g in range(groups):

        @pl.when(has_next)
        def _():
            kv_copy(g, reach, reach, me).wait_send()

        @pl.when(has_prior)
        def _():
            back_copy(g, reach).wait_send()

        for d in range(1, reach):
            _, _, straight = reached(d)
            _, exists, relays, _ = source_of(d)

            @pl.when(straight)
            def _():
                kv_copy(g, d, reach, me).wait_send()

            @pl.when(relays)
            def _():
                kv_pass(g, d).wait_send()

            @pl.when(exists)
            def _():
                back_copy(g, d).wait_send()


def on_device(ranges, groups, queries, keys, values, grad_out, doc_lengths):
    tokens = queries.shape[0]
    head_width = keys.shape[1] // groups
    reach = REACH * groups
    window = (reach + 1) * tokens
    anywhere = pl.BlockSpec(memory_space=pl.ANY)
    vmem = pl.BlockSpec(memory_space=pltpu.VMEM)
    dma = pltpu.SemaphoreType.DMA
    attended, grad_queries, grad_keys, grad_values = pl.pallas_call(
        functools.partial(kernel, ranges, groups, head_width),
        out_shape=(
            jax.ShapeDtypeStruct(queries.shape, BF16),
            jax.ShapeDtypeStruct(queries.shape, BF16),
            jax.ShapeDtypeStruct(keys.shape, BF16),
            jax.ShapeDtypeStruct(keys.shape, BF16),
        ),
        in_specs=[pl.BlockSpec(memory_space=pltpu.SMEM)] + [anywhere] * 4,
        out_specs=[vmem] * 4,
        scratch_shapes=[
            pltpu.VMEM(queries.shape, BF16),
            pltpu.VMEM(queries.shape, BF16),
            pltpu.VMEM((groups, window, 2 * head_width), BF16),
            pltpu.VMEM((2 * head_width, window), BF16),
            pltpu.VMEM((window, LANES), F32),
            pltpu.VMEM((window, LANES), F32),
            pltpu.VMEM((window, LANES), BF16),
            pltpu.VMEM((window, 2 * head_width), F32),
            pltpu.VMEM((groups, window, 2 * head_width), BF16),
            pltpu.VMEM((groups, reach * tokens, 2 * head_width), BF16),
            pltpu.VMEM((groups, reach * tokens, 2 * head_width), BF16),
            pltpu.VMEM((groups, tokens, 2 * head_width), F32),
            pltpu.VMEM(keys.shape, F32),
            pltpu.VMEM(keys.shape, F32),
            dma((2 * groups + 2,)),
            dma((groups, reach)),
            dma((groups, reach)),
            dma((groups, reach)),
            dma((groups, reach)),
            dma((groups, reach)),
            dma((groups, reach)),
        ],
        compiler_params=pltpu.CompilerParams(collective_id=0, has_side_effects=True),
    )(doc_lengths, queries, keys, values, grad_out)
    return attended, grad_queries, grad_keys, grad_values


def solution(mesh):
    rows = P(("ctx", "kvh"), None)
    return jax.shard_map(
        functools.partial(on_device, mesh.shape["ctx"], mesh.shape["kvh"]),
        mesh=mesh,
        in_specs=(rows, rows, rows, rows, P()),
        out_specs=(rows, rows, rows, rows),
        check_vma=False,
    )
```

time: 52.1 us -> 44.2 us (0.85)
  the two profiles are of different devices: /device:TPU:16 before, /device:TPU:20 now
where the time goes in v2:
time: 44.2 us; the launch traced here: 43.9 us
  Pallas kernels  39 us (88%)
  local copies, waits for them, and re-layouts  4.3 us (10%)
  between operations  0.65 us (1%)
    pallas_call x1, Pallas kernels, on_device(): pl.pallas_call(functools.partial(kernel, ranges, groups, head_width), out...  39 us
    unnamed x10, local copies, waits for them, and re-layouts  4.3 us

profile of v2, /device:TPU:20, one launch (start us, length us, event | category | flops | bytes accessed | tf_op | source)
XLA Modules:
  0.0 43.9 jit_solution(17282062524002820958)
XLA Ops:
  0.6 39.0 %shard_map.84 = (bf16[128,2048]{1,0:T(8,128)(2,1)}, bf16[128,2048]{1,0:T(8,128)(2,1)}, bf16[128,256]{1,0:T(8,128)(2,1)}, bf16[128,256]{1,0:T(8,128)(2,1)}) custom-call(s32[8]{0:T(128)} %doc_ref.1, bf16[128,2048]{1,0:T(8,128)(2,1)} %q_hbm.1, bf16[128,256]{1,0:T(8,128)(2,1)} %k_hbm.1, bf16[128,256]{1,0:T(8,128)(2,1)} %v_hbm.1, bf16[128,2048]{1,0:T(8,128)(2,1)} %do_hbm.1), custom_call_target="tpu_custom_call" | custom-call | tf_op jit(solution)/shard_map/pallas_call | solution.py:417
  39.6 0.0 copy-start
  39.6 1.9 %copy.13 = bf16[128,2048]{1,0:T(8,128)(2,1)} copy(bf16[128,2048]{1,0:T(8,128)(2,1)} %get-tuple-element.8) | data formatting | bytes 1048576
  41.6 0.0 copy-done
  41.6 0.0 copy-start.2
  41.6 0.8 %copy.14 = bf16[128,2048]{1,0:T(8,128)(2,1)} copy(bf16[128,2048]{1,0:T(8,128)(2,1)S(1)} %copy-done) | data formatting | bytes 1048576
  42.4 0.1 copy-done.2
  42.4 0.0 copy-start.1
  42.4 0.6 %copy.15 = bf16[128,256]{1,0:T(8,128)(2,1)} copy(bf16[128,256]{1,0:T(8,128)(2,1)S(1)} %copy-done.2) | data formatting | bytes 131072
  43.1 0.2 copy-done.1
  43.3 0.6 %copy.16 = bf16[128,256]{1,0:T(8,128)(2,1)} copy(bf16[128,256]{1,0:T(8,128)(2,1)S(1)} %copy-done.1) | data formatting | bytes 131072
Async XLA Ops:
  39.6 2.0 %copy-start = (bf16[128,2048]{1,0:T(8,128)(2,1)S(1)}, bf16[128,2048]{1,0:T(8,128)(2,1)}, u32[]{:S(2)}) copy-start(bf16[128,2048]{1,0:T(8,128)(2,1)} %get-tuple-element.9) | copy-start | bytes 1572868
  41.6 0.9 %copy-start.2 = (bf16[128,256]{1,0:T(8,128)(2,1)S(1)}, bf16[128,256]{1,0:T(8,128)(2,1)}, u32[]{:S(2)}) copy-start(bf16[128,256]{1,0:T(8,128)(2,1)} %get-tuple-element.10) | copy-start | bytes 196612
  42.4 0.9 %copy-start.1 = (bf16[128,256]{1,0:T(8,128)(2,1)S(1)}, bf16[128,256]{1,0:T(8,128)(2,1)}, u32[]{:S(2)}) copy-start(bf16[128,256]{1,0:T(8,128)(2,1)} %get-tuple-element.11) | copy-start | bytes 196612

commit v3 on v2

--- a/solution.py
+++ b/solution.py
@@ -24,7 +24,7 @@
 def kernel(
     ranges, groups, head_width, doc_ref, q_hbm, k_hbm, v_hbm, do_hbm,
     att_ref, gq_ref, gk_out, gv_out,
-    q_ref, do_ref, kv_ref, kvt_ref, bias_ref, s_ref, e_ref, acc_ref, out_ref, in_ref, pair_ref, prior_ref, gk_ref, gv_ref,
+    q_ref, do_ref, kv_ref, kvt_ref, bias_ref, s_bufs, e_bufs, acc_ref, out_ref, in_ref, pair_ref, prior_ref, gk_ref, gv_ref,
     load_sem, kv_send, kv_recv, pass_send, back_send, back_recv, pair_recv,
 ):
     tokens = q_ref.shape[0]
@@ -306,11 +306,11 @@
 
         acc_ref[...] = jnp.zeros_like(acc_ref)
 
-        def step(i, carry):
+        def step(i, carry, s_ref, e_ref):
             first_head = g * heads + i * per_step
 
             def head_columns(j):
-                return pl.ds(pl.multiple_of((first_head + j) * head_width, head_width), head_width)
+                return pl.ds((first_head + j) * head_width, head_width)
 
             def stacked(ref):
                 return jnp.concatenate([ref[:, head_columns(j)] for j in range(per_step)], axis=0)
@@ -349,14 +349,15 @@
                 gq_ref[:, head_columns(j)] = gq[j * tokens:(j + 1) * tokens]
             return carry
 
-        lax.fori_loop(0, steps - 1, step, 0)
+        for i in range(steps - 1):
+            step(i, 0, s_bufs.at[i % 2], e_bufs.at[i % 2])
         if g + 1 < groups:
             relay(g + 1)
         if g + 2 < groups:
             forward_prior(g + 2)
         if g > 0:
             send_pair_sums(g - 1)
-        lax.fori_loop(steps - 1, steps, step, 0)
+        step(steps - 1, 0, s_bufs.at[0], e_bufs.at[0])
         if g > 0:
             send_band_sums(g - 1)
 
@@ -430,8 +431,8 @@
             pltpu.VMEM((groups, window, 2 * head_width), BF16),
             pltpu.VMEM((2 * head_width, window), BF16),
             pltpu.VMEM((window, LANES), F32),
-            pltpu.VMEM((window, LANES), F32),
-            pltpu.VMEM((window, LANES), BF16),
+            pltpu.VMEM((2, window, LANES), F32),
+            pltpu.VMEM((2, window, LANES), BF16),
             pltpu.VMEM((window, 2 * head_width), F32),
             pltpu.VMEM((groups, window, 2 * head_width), BF16),
             pltpu.VMEM((groups, reach * tokens, 2 * head_width), BF16),

time: 44.2 us -> 42.4 us (0.959)
  Pallas kernels: 39 us -> 37.2 us
    pallas_call x1, Pallas kernels: 39 us -> 37.2 us  [on_device(): pl.pallas_call(functools.partial(kernel, ranges, groups, head_width), out...]
where the time goes in v3:
time: 42.4 us; the launch traced here: 42.2 us
  Pallas kernels  37.2 us (88%)
  local copies, waits for them, and re-layouts  4.3 us (10%)
  between operations  0.65 us (2%)
    pallas_call x1, Pallas kernels, on_device(): pl.pallas_call(functools.partial(kernel, ranges, groups, head_width), out...  37.2 us
    unnamed x10, local copies, waits for them, and re-layouts  4.3 us

profile of v3, /device:TPU:20, one launch (start us, length us, event | category | flops | bytes accessed | tf_op | source)
XLA Modules:
  0.0 42.2 jit_solution(11871039208471742050)
XLA Ops:
  0.6 37.2 %shard_map.84 = (bf16[128,2048]{1,0:T(8,128)(2,1)}, bf16[128,2048]{1,0:T(8,128)(2,1)}, bf16[128,256]{1,0:T(8,128)(2,1)}, bf16[128,256]{1,0:T(8,128)(2,1)}) custom-call(s32[8]{0:T(128)} %doc_ref.1, bf16[128,2048]{1,0:T(8,128)(2,1)} %q_hbm.1, bf16[128,256]{1,0:T(8,128)(2,1)} %k_hbm.1, bf16[128,256]{1,0:T(8,128)(2,1)} %v_hbm.1, bf16[128,2048]{1,0:T(8,128)(2,1)} %do_hbm.1), custom_call_target="tpu_custom_call" | custom-call | tf_op jit(solution)/shard_map/pallas_call | solution.py:418
  37.9 0.0 copy-start
  37.9 1.9 %copy.13 = bf16[128,2048]{1,0:T(8,128)(2,1)} copy(bf16[128,2048]{1,0:T(8,128)(2,1)} %get-tuple-element.8) | data formatting | bytes 1048576
  39.8 0.0 copy-done
  39.8 0.0 copy-start.2
  39.8 0.8 %copy.14 = bf16[128,2048]{1,0:T(8,128)(2,1)} copy(bf16[128,2048]{1,0:T(8,128)(2,1)S(1)} %copy-done) | data formatting | bytes 1048576
  40.6 0.1 copy-done.2
  40.7 0.0 copy-start.1
  40.7 0.6 %copy.15 = bf16[128,256]{1,0:T(8,128)(2,1)} copy(bf16[128,256]{1,0:T(8,128)(2,1)S(1)} %copy-done.2) | data formatting | bytes 131072
  41.3 0.2 copy-done.1
  41.6 0.6 %copy.16 = bf16[128,256]{1,0:T(8,128)(2,1)} copy(bf16[128,256]{1,0:T(8,128)(2,1)S(1)} %copy-done.1) | data formatting | bytes 131072
Async XLA Ops:
  37.9 2.0 %copy-start = (bf16[128,2048]{1,0:T(8,128)(2,1)S(1)}, bf16[128,2048]{1,0:T(8,128)(2,1)}, u32[]{:S(2)}) copy-start(bf16[128,2048]{1,0:T(8,128)(2,1)} %get-tuple-element.9) | copy-start | bytes 1572868
  39.8 0.9 %copy-start.2 = (bf16[128,256]{1,0:T(8,128)(2,1)S(1)}, bf16[128,256]{1,0:T(8,128)(2,1)}, u32[]{:S(2)}) copy-start(bf16[128,256]{1,0:T(8,128)(2,1)} %get-tuple-element.10) | copy-start | bytes 196612
  40.7 0.9 %copy-start.1 = (bf16[128,256]{1,0:T(8,128)(2,1)S(1)}, bf16[128,256]{1,0:T(8,128)(2,1)}, u32[]{:S(2)}) copy-start(bf16[128,256]{1,0:T(8,128)(2,1)} %get-tuple-element.11) | copy-start | bytes 196612
